TPU v7x, 128 devices: a whole 4x4x4 slice. The times are simulated.
128 devices in a mesh: gx: 16 (over z, y), gy: 8 (over x, core).
Axes of the slice: x: 4, y: 4, z: 4, core: 2. Of those that a mesh axis runs over, the one named last changes fastest.
Arguments:
- centers: float32 [3, 262144], P(None, ('gx', 'gy')), may hold values from -6 to 6
- tilt_angle: float32 [262144], P(('gx', 'gy')), may hold values from -3.140625 to 3.140625
- turn_angle: float32 [262144], P(('gx', 'gy')), may hold values from -3.140625 to 3.140625
- radius: float32 [262144], P(('gx', 'gy')), may hold values from 0.5 to 2
- mobility_perp: float32 [262144], P(('gx', 'gy')), may hold values from 0.3 to 3
- mobility_axial: float32 [262144], P(('gx', 'gy')), may hold values from 0.2 to 2
- mobility_rot: float32 [262144], P(('gx', 'gy')), may hold values from 0.3 to 3
- external_load: float32 [6, 262144], P(None, ('gx', 'gy')), may hold values from -60 to 60
- local_first: int32 [327680], P(('gx', 'gy')), may hold values from 0 to 2047, as said below
- local_second: int32 [327680], P(('gx', 'gy')), may hold values from 0 to 2047
- arc_first: float32 [327680], P(('gx', 'gy')), may hold values from -1 to 1
- arc_second: float32 [327680], P(('gx', 'gy')), may hold values from -1 to 1
- cross_mine: int32 [128, 4, 256], P(('gx', 'gy')), may hold values from 0 to 2047
- cross_slot: int32 [128, 4, 256], P(('gx', 'gy')), may hold values from 0 to 127
- cross_arc_own: float32 [128, 4, 256], P(('gx', 'gy')), may hold values from -1 to 1
- cross_arc_other: float32 [128, 4, 256], P(('gx', 'gy')), may hold values from -1 to 1
- cross_count: int32 [128, 4], P(('gx', 'gy')), may hold values from 0 to 256, as said below
- export_rows: int32 [128, 4, 128], P(('gx', 'gy')), may hold values from 0 to 2047
Outputs:
- velocity: float32 [6, 262144], P(None, ('gx', 'gy'))
- force_local: float32 [327680], P(('gx', 'gy'))
- force_cross: float32 [128, 4, 256], P(('gx', 'gy'))
Inputs may be any that keep to these rules, and one draw needn't show every extreme that they name: local_second never equals local_first of the same pair. Slots c < cross_count[k, d] are live, the others dead. A direction whose partner lies outside the mesh has count 0. In every draw some block holds 256 live pairs.
All inputs are finite; a program needn't handle non-finite values.
Results may differ from a plain program's by a relative error of at most 0.00002.
Values sent between devices are 32-bit elements; how exact they have to be, the bound alone decides.
A program may use at most 64 MiB of HBM per device.

v0:
```python
import jax
import jax.numpy as jnp
from jax import lax
from jax.sharding import PartitionSpec as P

step_time = 0.5
floor_gap = 0.25
tiny = 1e-06


def passed_along(shard, axis, by):
    devices = lax.axis_size(axis)
    pairs = [(i, i + by) for i in range(devices) if 0 <= i + by < devices]
    return lax.ppermute(shard, axis, pairs)


def tangent_of(polar, azimuth):
    lifted = jnp.sin(polar)
    return jnp.stack([lifted * jnp.cos(azimuth), lifted * jnp.sin(azimuth), jnp.cos(polar)])


def cross_product(left, right):
    return jnp.stack(
        [
            left[1] * right[2] - left[2] * right[1],
            left[2] * right[0] - left[0] * right[2],
            left[0] * right[1] - left[1] * right[0],
        ]
    )


def pair_terms(geo_first, geo_second, arc_one, arc_two, live_mask):
    lever_first = arc_one * tangent_of(geo_first[3], geo_first[4])
    lever_second = arc_two * tangent_of(geo_second[3], geo_second[4])
    apart = geo_first[:3] + lever_first - geo_second[:3] - lever_second
    spacing = jnp.sqrt(jnp.sum(apart * apart, axis=0))
    normal = apart / jnp.maximum(spacing, floor_gap) * live_mask
    jacobian = jnp.concatenate(
        [normal, cross_product(lever_first, normal), cross_product(lever_second, normal)], axis=0
    )
    clearance = (spacing - geo_first[5] - geo_second[5]) * live_mask
    return (jacobian, clearance)


def rate_of(jacobian, moving_first, moving_second):
    return (
        jnp.sum(jacobian[:3] * (moving_first[:3] - moving_second[:3]), axis=0)
        + jnp.sum(jacobian[3:6] * moving_first[3:], axis=0)
        - jnp.sum(jacobian[6:] * moving_second[3:], axis=0)
    )


def push_terms(jacobian, amount):
    return (amount * jacobian[:6], -amount * jnp.concatenate([jacobian[:3], jacobian[6:]], axis=0))


def apply_mobility(applied, tangent, perp, axial, rotary):
    force = applied[:3]
    along = jnp.sum(tangent * force, axis=0)
    return jnp.concatenate([perp * force + axial * along * tangent, rotary * applied[3:]], axis=0)


def toward_owner(blocks):
    across = lax.axis_size("gy")
    received = []
    for position, offset in enumerate((1, across + 1, across, across - 1)):
        received.append(passed_along(blocks[position], ("gx", "gy"), -offset))
    return jnp.stack(received)


def toward_partner(blocks):
    across = lax.axis_size("gy")
    received = []
    for position, offset in enumerate((1, across + 1, across, across - 1)):
        received.append(passed_along(blocks[position], ("gx", "gy"), offset))
    return jnp.stack(received)


def sum_pairs(first_term, second_term):
    return lax.psum((first_term, second_term), ("gx", "gy"))


def on_device(
    centers,
    tilt_angle,
    turn_angle,
    radius,
    mobility_perp,
    mobility_axial,
    mobility_rot,
    external_load,
    local_first,
    local_second,
    arc_first,
    arc_second,
    cross_mine,
    cross_slot,
    cross_arc_own,
    cross_arc_other,
    cross_count,
    export_rows,
):
    seg_rows = centers.shape[1]
    local_pairs = local_first.shape[0]
    blocks_cap = cross_mine.shape[2]
    export_cap = export_rows.shape[2]
    geometry = jnp.concatenate([centers, tilt_angle[None], turn_angle[None], radius[None]], axis=0)
    tangent = tangent_of(tilt_angle, turn_angle)
    exported = export_rows[0]
    export_flat = exported.reshape(-1)
    own_rows = cross_mine[0].reshape(-1)
    all_rows = jnp.concatenate([local_first, local_second, own_rows])
    slot_flat = (cross_slot[0] + (jnp.arange(4, dtype=jnp.int32) * export_cap)[:, None]).reshape(-1)
    live_mask = (
        (jnp.arange(blocks_cap, dtype=jnp.int32)[None, :] < cross_count[0][:, None])
        .astype(jnp.float32)
        .reshape(-1)
    )

    def picked(source):
        taken = jnp.take(source, all_rows, axis=1)
        return (
            taken[:, :local_pairs],
            taken[:, local_pairs : 2 * local_pairs],
            taken[:, 2 * local_pairs :],
        )

    def outgoing(source):
        return jnp.moveaxis(jnp.take(source, exported, axis=1), 1, 0)

    def incoming(blocks):
        flattened = jnp.moveaxis(blocks, 0, 1).reshape(blocks.shape[1], -1)
        return jnp.take(flattened, slot_flat, axis=1)

    def mobile(applied):
        return apply_mobility(applied, tangent, mobility_perp, mobility_axial, mobility_rot)

    drift = mobile(external_load)
    remote_geometry = incoming(toward_owner(outgoing(geometry)))
    geo_one, geo_two, geo_own = picked(geometry)
    jacobian_local, clearance_local = pair_terms(geo_one, geo_two, arc_first, arc_second, 1.0)
    jacobian_cross, clearance_cross = pair_terms(
        geo_own,
        remote_geometry,
        cross_arc_own[0].reshape(-1),
        cross_arc_other[0].reshape(-1),
        live_mask,
    )

    def spread(amount_local, amount_cross):
        local_one, local_two = push_terms(jacobian_local, amount_local)
        cross_one, cross_two = push_terms(jacobian_cross, amount_cross)
        slot_loads = jnp.zeros((6, 4 * export_cap), jnp.float32).at[:, slot_flat].add(cross_two)
        returned = toward_partner(jnp.moveaxis(slot_loads.reshape(6, 4, export_cap), 1, 0))
        pushes = jnp.concatenate([local_one, local_two, cross_one], axis=1)
        loads = jnp.zeros((6, seg_rows), jnp.float32).at[:, all_rows].add(pushes)
        return loads.at[:, export_flat].add(jnp.moveaxis(returned, 0, 1).reshape(6, -1))

    def rates(moving, remote_moving=None):
        remote_moving = incoming(toward_owner(outgoing(moving)))
        move_one, move_two, move_own = picked(moving)
        rate_local = rate_of(jacobian_local, move_one, move_two)
        rate_cross = rate_of(jacobian_cross, move_own, remote_moving)
        return (rate_local, rate_cross)

    drift_local, drift_cross = rates(drift, None)
    slope_local = clearance_local / step_time + drift_local
    slope_cross = clearance_cross / step_time + drift_cross
    top_first = jnp.sum(slope_local * slope_local) + jnp.sum(slope_cross * slope_cross)
    loads_first = spread(slope_local, slope_cross)
    moved_first = mobile(loads_first)
    curved_local, curved_cross = rates(moved_first)
    top_first, bottom_first = sum_pairs(
        top_first, jnp.sum(slope_local * curved_local) + jnp.sum(slope_cross * curved_cross)
    )
    step_first = top_first / (bottom_first + tiny)
    thrust_local = jnp.maximum(0.0, -step_first * slope_local)
    thrust_cross = jnp.maximum(0.0, -step_first * slope_cross)
    loads_second = spread(thrust_local, thrust_cross)
    moved_second = mobile(loads_second)
    moving_one = drift + moved_second
    top_second = jnp.sum(thrust_local * thrust_local) + jnp.sum(thrust_cross * thrust_cross)
    rate_local, rate_cross = rates(moving_one)
    next_local = clearance_local / step_time + rate_local
    next_cross = clearance_cross / step_time + rate_cross
    top_second, bottom_second = sum_pairs(
        top_second,
        jnp.sum(thrust_local * (next_local - slope_local))
        + jnp.sum(thrust_cross * (next_cross - slope_cross)),
    )
    step_second = top_second / (bottom_second + tiny)
    force_local = jnp.maximum(0.0, thrust_local - step_second * next_local)
    force_cross = jnp.maximum(0.0, thrust_cross - step_second * next_cross)
    velocity = drift + mobile(spread(force_local, force_cross))
    return (velocity, force_local, force_cross.reshape(1, 4, blocks_cap))


def solution(mesh):
    return jax.shard_map(
        on_device,
        mesh=mesh,
        in_specs=(
            P(None, ("gx", "gy")),
            P(("gx", "gy")),
            P(("gx", "gy")),
            P(("gx", "gy")),
            P(("gx", "gy")),
            P(("gx", "gy")),
            P(("gx", "gy")),
            P(None, ("gx", "gy")),
            P(("gx", "gy")),
            P(("gx", "gy")),
            P(("gx", "gy")),
            P(("gx", "gy")),
            P(("gx", "gy"), None, None),
            P(("gx", "gy"), None, None),
            P(("gx", "gy"), None, None),
            P(("gx", "gy"), None, None),
            P(("gx", "gy"), None),
            P(("gx", "gy"), None, None),
        ),
        out_specs=(P(None, ("gx", "gy")), P(("gx", "gy")), P(("gx", "gy"), None, None)),
        check_vma=False,
    )
```

profile of v0, /device:TPU:1, one launch (start us, length us, event | category | flops | bytes accessed | tf_op | source)
XLA Modules:
  0.0 529.1 jit_solution(2936644011537897512)
XLA Ops:
  11.4 3.3 collective-permute-start
  23.0 20.9 %gather_fusion.1 = f32[6144,6]{1,0:T(8,128)} fusion(f32[6,2048]{0,1:T(8,128)S(1)} %copy.319, s32[6144]{0:T(1024)S(1)} %fusion.33), kind=kCustom, calls=%fused_computation.3.clone | custom fusion | bytes 319488 | tf_op jit(solution)/shard_map/jit(_take)/gather | solution.py:121
  43.9 20.9 %gather_fusion = f32[6144,6]{1,0:T(8,128)} fusion(f32[6,2048]{0,1:T(8,128)S(1)} %copy.317, s32[6144]{0:T(1024)S(1)} %fusion.33), kind=kCustom, calls=%fused_computation.clone | custom fusion | bytes 319488 | tf_op jit(solution)/shard_map/jit(_take)/gather | solution.py:121
  88.5 3.3 gather_fusion.3
  94.6 2.8 gather_fusion.5
  100.2 6.1 %scatter_custom_fusion.1 = f32[6,512]{0,1:T(8,128)S(1)} fusion(s32[1024]{0:T(1024)S(1)} %bitcast.296, f32[1024,6]{1,0:T(8,128)S(1)} %copy.336, f32[]{:T(128)} %constant.32.clone.1), kind=kCustom, calls=%fused_computation.39 | custom fusion | flops 6144 | bytes 12292 | tf_op jit(solution)/shard_map/scatter-add | solution.py:153
  106.4 4.1 collective-permute-start.8
  110.4 5.0 collective-permute-start.9
  115.5 5.1 collective-permute-start.10
  120.6 6.2 %collective-permute-start.11 = (f32[6,128]{1,0:T(8,128)S(1)}, f32[6,128]{1,0:T(8,128)S(1)}, u32[]{:S(2)}, u32[]{:S(2)}) collective-permute-start(f32[6,128]{1,0:T(8,128)S(1)} %get-tuple-element.130), channel_id=1, source_target_pairs={{0,7},{1,8},{2,9},{3,10},{4,11},{5,12},{6,13},{7,14},{8,15},{9,16}... | collective-permute-start | bytes 9224 | tf_op jit(solution)/shard_map/ppermute | solution.py:14
  130.8 33.7 %scatter_custom_fusion = f32[6,2048]{0,1:T(8,128)S(1)} fusion(s32[6144]{0:T(1024)S(1)} %bitcast.275, f32[6144,6]{1,0:T(8,128)} %copy.335, f32[]{:T(128)} %constant.32.clone.1), kind=kCustom, calls=%fused_computation.25 | custom fusion | flops 36864 | bytes 49664 | tf_op jit(solution)/shard_map/scatter-add | solution.py:156
  164.9 4.2 scatter_fusion
  171.8 20.9 %gather_fusion.6 = f32[6144,6]{1,0:T(8,128)} fusion(f32[6,2048]{0,1:T(8,128)S(1)} %copy.344, s32[6144]{0:T(1024)S(1)} %copy-done.4), kind=kCustom, calls=%fused_computation.4.clone | custom fusion | bytes 319488 | tf_op jit(solution)/shard_map/jit(_take)/gather | solution.py:121
  192.9 3.2 collective-permute-start.12
  204.3 4.1 collective-permute-done.15
  208.6 2.8 gather_fusion.8
  215.5 74.8 %all-reduce.1 = (f32[]{:T(128)}, f32[]{:T(128)}) all-reduce(f32[]{:T(128)S(6)} %add.310, f32[]{:T(128)S(6)} %add.319), channel_id=1, replica_groups=mesh['gx'=16,'gy'=8] {'gx','gy'}, use_global_device_ids=true, to_apply=%region_11.15 | all-reduce | flops 2 | bytes 16 | tf_op jit(solution)/shard_map/psum | solution.py:80
  291.9 6.2 %scatter_custom_fusion.4 = f32[6,512]{0,1:T(8,128)S(1)} fusion(s32[1024]{0:T(1024)} %bitcast.297, f32[1024,6]{1,0:T(8,128)S(1)} %copy.354, f32[]{:T(128)} %constant.32.clone.1), kind=kCustom, calls=%fused_computation.37 | custom fusion | flops 6144 | bytes 12800 | tf_op jit(solution)/shard_map/scatter-add | solution.py:153
  298.2 3.8 collective-permute-start.16
  303.4 3.1 collective-permute-start.18
  306.5 2.8 collective-permute-start.19
  311.8 33.7 %scatter_custom_fusion.3 = f32[6,2048]{0,1:T(8,128)S(1)} fusion(s32[6144]{0:T(1024)} %bitcast.276, f32[6144,6]{1,0:T(8,128)} %copy.353, f32[]{:T(128)} %constant.32.clone.1), kind=kCustom, calls=%fused_computation.23 | custom fusion | flops 36864 | bytes 49664 | tf_op jit(solution)/shard_map/scatter-add | solution.py:156
  345.8 3.9 scatter_fusion.1
  351.4 20.9 %gather_fusion.9 = f32[6144,6]{1,0:T(8,128)} fusion(f32[6,2048]{0,1:T(8,128)S(1)} %copy.362, s32[6144]{0:T(1024)S(1)} %copy-done.4), kind=kCustom, calls=%fused_computation.5.clone | custom fusion | bytes 319488 | tf_op jit(solution)/shard_map/jit(_take)/gather | solution.py:121
  376.3 4.9 collective-permute-start.20
  387.1 3.7 collective-permute-done.23
  391.0 2.8 gather_fusion.11
  397.4 68.4 %all-reduce = (f32[]{:T(128)}, f32[]{:T(128)}) all-reduce(f32[]{:T(128)S(6)} %add.321, f32[]{:T(128)S(6)} %add.328), channel_id=1, replica_groups=mesh['gx'=16,'gy'=8] {'gx','gy'}, use_global_device_ids=true, to_apply=%region_27.31 | all-reduce | flops 2 | bytes 16 | tf_op jit(solution)/shard_map/psum | solution.py:80
  468.0 6.2 %scatter_custom_fusion.7 = f32[6,512]{0,1:T(8,128)S(1)} fusion(s32[1024]{0:T(1024)} %bitcast.298, f32[1024,6]{1,0:T(8,128)S(1)} %copy.372, f32[]{:T(128)} %constant.32.clone.1), kind=kCustom, calls=%fused_computation.35 | custom fusion | flops 6144 | bytes 12800 | tf_op jit(solution)/shard_map/scatter-add | solution.py:153
  480.9 5.0 collective-permute-start.27
  489.1 33.7 %scatter_custom_fusion.6 = f32[6,2048]{0,1:T(8,128)S(1)} fusion(s32[6144]{0:T(1024)} %bitcast.277, f32[6144,6]{1,0:T(8,128)} %copy.371, f32[]{:T(128)} %constant.32.clone.1), kind=kCustom, calls=%fused_computation.21 | custom fusion | flops 36864 | bytes 49664 | tf_op jit(solution)/shard_map/scatter-add | solution.py:156
  523.1 3.9 scatter_fusion.2
  (395 shorter events, 93.7 us)
Async XLA Ops:
  11.4 70.4 %collective-permute-start = (f32[6,128]{1,0:T(8,128)}, f32[6,128]{1,0:T(8,128)}, u32[]{:S(2)}, u32[]{:S(2)}) collective-permute-start(f32[6,128]{1,0:T(8,128)} %get-tuple-element.141), channel_id=1, source_target_pairs={{1,0},{2,1},{3,2},{4,3},{5,4},{6,5},{7,6},{8,7},{9,8},{10,9},{11,1... | collective-permute-start | bytes 9224 | tf_op jit(solution)/shard_map/ppermute | solution.py:14
  14.7 69.1 %collective-permute-start.1 = (f32[6,128]{1,0:T(8,128)}, f32[6,128]{1,0:T(8,128)}, u32[]{:S(2)}, u32[]{:S(2)}) collective-permute-start(f32[6,128]{1,0:T(8,128)} %get-tuple-element.144), channel_id=1, source_target_pairs={{9,0},{10,1},{11,2},{12,3},{13,4},{14,5},{15,6},{16,7},{17,8},{18,... | collective-permute-start | bytes 9224 | tf_op jit(solution)/shard_map/ppermute | solution.py:14
  16.0 69.7 %collective-permute-start.2 = (f32[6,128]{1,0:T(8,128)}, f32[6,128]{1,0:T(8,128)}, u32[]{:S(2)}, u32[]{:S(2)}) collective-permute-start(f32[6,128]{1,0:T(8,128)} %get-tuple-element.143), channel_id=1, source_target_pairs={{8,0},{9,1},{10,2},{11,3},{12,4},{13,5},{14,6},{15,7},{16,8},{17,9... | collective-permute-start | bytes 9224 | tf_op jit(solution)/shard_map/ppermute | solution.py:14
  17.3 70.4 %collective-permute-start.3 = (f32[6,128]{1,0:T(8,128)}, f32[6,128]{1,0:T(8,128)}, u32[]{:S(2)}, u32[]{:S(2)}) collective-permute-start(f32[6,128]{1,0:T(8,128)} %get-tuple-element.142), channel_id=1, source_target_pairs={{7,0},{8,1},{9,2},{10,3},{11,4},{12,5},{13,6},{14,7},{15,8},{16,9}... | collective-permute-start | bytes 9224 | tf_op jit(solution)/shard_map/ppermute | solution.py:14
  19.2 72.9 %collective-permute-start.4 = (f32[6,128]{1,0:T(8,128)}, f32[6,128]{1,0:T(8,128)}, u32[]{:S(2)}, u32[]{:S(2)}) collective-permute-start(f32[6,128]{1,0:T(8,128)} %get-tuple-element.137), channel_id=1, source_target_pairs={{1,0},{2,1},{3,2},{4,3},{5,4},{6,5},{7,6},{8,7},{9,8},{10,9},{11,1... | collective-permute-start | bytes 9224 | tf_op jit(solution)/shard_map/ppermute | solution.py:14
  81.7 11.0 %collective-permute-start.5 = (f32[6,128]{1,0:T(8,128)}, f32[6,128]{1,0:T(8,128)S(1)}, u32[]{:S(2)}, u32[]{:S(2)}) collective-permute-start(f32[6,128]{1,0:T(8,128)} %get-tuple-element.140), channel_id=1, source_target_pairs={{9,0},{10,1},{11,2},{12,3},{13,4},{14,5},{15,6},{16,7},{17,8},{18,... | collective-permute-start | bytes 9224 | tf_op jit(solution)/shard_map/ppermute | solution.py:14
  83.7 9.0 %collective-permute-start.6 = (f32[6,128]{1,0:T(8,128)}, f32[6,128]{1,0:T(8,128)S(1)}, u32[]{:S(2)}, u32[]{:S(2)}) collective-permute-start(f32[6,128]{1,0:T(8,128)} %get-tuple-element.139), channel_id=1, source_target_pairs={{8,0},{9,1},{10,2},{11,3},{12,4},{13,5},{14,6},{15,7},{16,8},{17,9... | collective-permute-start | bytes 9224 | tf_op jit(solution)/shard_map/ppermute | solution.py:14
  85.7 8.7 %collective-permute-start.7 = (f32[6,128]{1,0:T(8,128)}, f32[6,128]{1,0:T(8,128)S(1)}, u32[]{:S(2)}, u32[]{:S(2)}) collective-permute-start(f32[6,128]{1,0:T(8,128)} %get-tuple-element.138), channel_id=1, source_target_pairs={{7,0},{8,1},{9,2},{10,3},{11,4},{12,5},{13,6},{14,7},{15,8},{16,9}... | collective-permute-start | bytes 9224 | tf_op jit(solution)/shard_map/ppermute | solution.py:14
  106.4 58.2 %collective-permute-start.8 = (f32[6,128]{1,0:T(8,128)S(1)}, f32[6,128]{1,0:T(8,128)S(1)}, u32[]{:S(2)}, u32[]{:S(2)}) collective-permute-start(f32[6,128]{1,0:T(8,128)S(1)} %get-tuple-element.129), channel_id=1, source_target_pairs={{0,1},{1,2},{2,3},{3,4},{4,5},{5,6},{6,7},{7,8},{8,9},{9,10},{10,1... | collective-permute-start | bytes 9224 | tf_op jit(solution)/shard_map/ppermute | solution.py:14
  110.4 54.2 %collective-permute-start.9 = (f32[6,128]{1,0:T(8,128)S(1)}, f32[6,128]{1,0:T(8,128)S(1)}, u32[]{:S(2)}, u32[]{:S(2)}) collective-permute-start(f32[6,128]{1,0:T(8,128)S(1)} %get-tuple-element.132), channel_id=1, source_target_pairs={{0,9},{1,10},{2,11},{3,12},{4,13},{5,14},{6,15},{7,16},{8,17},{9,1... | collective-permute-start | bytes 9224 | tf_op jit(solution)/shard_map/ppermute | solution.py:14
  115.5 49.2 %collective-permute-start.10 = (f32[6,128]{1,0:T(8,128)S(1)}, f32[6,128]{1,0:T(8,128)S(1)}, u32[]{:S(2)}, u32[]{:S(2)}) collective-permute-start(f32[6,128]{1,0:T(8,128)S(1)} %get-tuple-element.131), channel_id=1, source_target_pairs={{0,8},{1,9},{2,10},{3,11},{4,12},{5,13},{6,14},{7,15},{8,16},{9,17... | collective-permute-start | bytes 9224 | tf_op jit(solution)/shard_map/ppermute | solution.py:14
  120.6 44.1 %collective-permute-start.11 = (f32[6,128]{1,0:T(8,128)S(1)}, f32[6,128]{1,0:T(8,128)S(1)}, u32[]{:S(2)}, u32[]{:S(2)}) collective-permute-start(f32[6,128]{1,0:T(8,128)S(1)} %get-tuple-element.130), channel_id=1, source_target_pairs={{0,7},{1,8},{2,9},{3,10},{4,11},{5,12},{6,13},{7,14},{8,15},{9,16}... | collective-permute-start | bytes 9224 | tf_op jit(solution)/shard_map/ppermute | solution.py:14
  192.9 11.0 %collective-permute-start.12 = (f32[6,128]{1,0:T(8,128)S(1)}, f32[6,128]{1,0:T(8,128)S(1)}, u32[]{:S(2)}, u32[]{:S(2)}) collective-permute-start(f32[6,128]{1,0:T(8,128)S(1)} %get-tuple-element.125), channel_id=1, source_target_pairs={{1,0},{2,1},{3,2},{4,3},{5,4},{6,5},{7,6},{8,7},{9,8},{10,9},{11,1... | collective-permute-start | bytes 9224 | tf_op jit(solution)/shard_map/ppermute | solution.py:14
  196.1 7.8 %collective-permute-start.13 = (f32[6,128]{1,0:T(8,128)S(1)}, f32[6,128]{1,0:T(8,128)S(1)}, u32[]{:S(2)}, u32[]{:S(2)}) collective-permute-start(f32[6,128]{1,0:T(8,128)S(1)} %get-tuple-element.128), channel_id=1, source_target_pairs={{9,0},{10,1},{11,2},{12,3},{13,4},{14,5},{15,6},{16,7},{17,8},{18,... | collective-permute-start | bytes 9224 | tf_op jit(solution)/shard_map/ppermute | solution.py:14
  197.4 6.9 %collective-permute-start.14 = (f32[6,128]{1,0:T(8,128)S(1)}, f32[6,128]{1,0:T(8,128)S(1)}, u32[]{:S(2)}, u32[]{:S(2)}) collective-permute-start(f32[6,128]{1,0:T(8,128)S(1)} %get-tuple-element.127), channel_id=1, source_target_pairs={{8,0},{9,1},{10,2},{11,3},{12,4},{13,5},{14,6},{15,7},{16,8},{17,9... | collective-permute-start | bytes 9224 | tf_op jit(solution)/shard_map/ppermute | solution.py:14
  198.7 110.7 %copy-start.49 = (f32[1,2560]{1,0:T(1,128)S(1)}, f32[1,2560]{1,0:T(1,128)}, u32[]{:S(2)}) copy-start(f32[1,2560]{1,0:T(1,128)} %get-tuple-element.61) | copy-start | bytes 30724
  198.7 9.7 %collective-permute-start.15 = (f32[6,128]{1,0:T(8,128)S(1)}, f32[6,128]{1,0:T(8,128)S(1)}, u32[]{:S(2)}, u32[]{:S(2)}) collective-permute-start(f32[6,128]{1,0:T(8,128)S(1)} %get-tuple-element.126), channel_id=1, source_target_pairs={{7,0},{8,1},{9,2},{10,3},{11,4},{12,5},{13,6},{14,7},{15,8},{16,9}... | collective-permute-start | bytes 9224 | tf_op jit(solution)/shard_map/ppermute | solution.py:14
  298.2 47.3 %collective-permute-start.16 = (f32[6,128]{1,0:T(8,128)S(1)}, f32[6,128]{1,0:T(8,128)S(1)}, u32[]{:S(2)}, u32[]{:S(2)}) collective-permute-start(f32[6,128]{1,0:T(8,128)S(1)} %get-tuple-element.119), channel_id=1, source_target_pairs={{0,1},{1,2},{2,3},{3,4},{4,5},{5,6},{6,7},{7,8},{8,9},{9,10},{10,1... | collective-permute-start | bytes 9224 | tf_op jit(solution)/shard_map/ppermute | solution.py:14
  302.1 43.5 %collective-permute-start.17 = (f32[6,128]{1,0:T(8,128)S(1)}, f32[6,128]{1,0:T(8,128)S(1)}, u32[]{:S(2)}, u32[]{:S(2)}) collective-permute-start(f32[6,128]{1,0:T(8,128)S(1)} %get-tuple-element.122), channel_id=1, source_target_pairs={{0,9},{1,10},{2,11},{3,12},{4,13},{5,14},{6,15},{7,16},{8,17},{9,1... | collective-permute-start | bytes 9224 | tf_op jit(solution)/shard_map/ppermute | solution.py:14
  303.4 42.2 %collective-permute-start.18 = (f32[6,128]{1,0:T(8,128)S(1)}, f32[6,128]{1,0:T(8,128)S(1)}, u32[]{:S(2)}, u32[]{:S(2)}) collective-permute-start(f32[6,128]{1,0:T(8,128)S(1)} %get-tuple-element.121), channel_id=1, source_target_pairs={{0,8},{1,9},{2,10},{3,11},{4,12},{5,13},{6,14},{7,15},{8,16},{9,17... | collective-permute-start | bytes 9224 | tf_op jit(solution)/shard_map/ppermute | solution.py:14
  306.5 39.1 %collective-permute-start.19 = (f32[6,128]{1,0:T(8,128)S(1)}, f32[6,128]{1,0:T(8,128)S(1)}, u32[]{:S(2)}, u32[]{:S(2)}) collective-permute-start(f32[6,128]{1,0:T(8,128)S(1)} %get-tuple-element.120), channel_id=1, source_target_pairs={{0,7},{1,8},{2,9},{3,10},{4,11},{5,12},{6,13},{7,14},{8,15},{9,16}... | collective-permute-start | bytes 9224 | tf_op jit(solution)/shard_map/ppermute | solution.py:14
  373.5 112.4 %copy-start.50 = (f32[1,2560]{1,0:T(1,128)S(1)}, f32[1,2560]{1,0:T(1,128)}, u32[]{:S(2)}) copy-start(f32[1,2560]{1,0:T(1,128)} %get-tuple-element.61) | copy-start | bytes 30724
  373.5 112.4 %copy-start.55 = (f32[1,2560]{1,0:T(1,128)S(1)}, f32[1,2560]{1,0:T(1,128)}, u32[]{:S(2)}) copy-start(f32[1,2560]{1,0:T(1,128)} %get-tuple-element.62) | copy-start | bytes 30724
  375.9 110.2 %copy-start.67 = (f32[1,4,256]{2,1,0:T(4,128)S(1)}, f32[1,4,256]{2,1,0:T(4,128)}, u32[]{:S(2)}) copy-start(f32[1,4,256]{2,1,0:T(4,128)} %sqrt.64) | copy-start | bytes 12292
  376.3 9.5 %collective-permute-start.20 = (f32[6,128]{1,0:T(8,128)S(1)}, f32[6,128]{1,0:T(8,128)S(1)}, u32[]{:S(2)}, u32[]{:S(2)}) collective-permute-start(f32[6,128]{1,0:T(8,128)S(1)} %get-tuple-element.115), channel_id=1, source_target_pairs={{1,0},{2,1},{3,2},{4,3},{5,4},{6,5},{7,6},{8,7},{9,8},{10,9},{11,1... | collective-permute-start | bytes 9224 | tf_op jit(solution)/shard_map/ppermute | solution.py:14
  381.3 5.8 %collective-permute-start.21 = (f32[6,128]{1,0:T(8,128)S(1)}, f32[6,128]{1,0:T(8,128)S(1)}, u32[]{:S(2)}, u32[]{:S(2)}) collective-permute-start(f32[6,128]{1,0:T(8,128)S(1)} %get-tuple-element.118), channel_id=1, source_target_pairs={{9,0},{10,1},{11,2},{12,3},{13,4},{14,5},{15,6},{16,7},{17,8},{18,... | collective-permute-start | bytes 9224 | tf_op jit(solution)/shard_map/ppermute | solution.py:14
  382.6 4.5 collective-permute-start.22
  383.9 6.9 %collective-permute-start.23 = (f32[6,128]{1,0:T(8,128)S(1)}, f32[6,128]{1,0:T(8,128)S(1)}, u32[]{:S(2)}, u32[]{:S(2)}) collective-permute-start(f32[6,128]{1,0:T(8,128)S(1)} %get-tuple-element.116), channel_id=1, source_target_pairs={{7,0},{8,1},{9,2},{10,3},{11,4},{12,5},{13,6},{14,7},{15,8},{16,9}... | collective-permute-start | bytes 9224 | tf_op jit(solution)/shard_map/ppermute | solution.py:14
  474.4 48.5 %collective-permute-start.24 = (f32[6,128]{1,0:T(8,128)S(1)}, f32[6,128]{1,0:T(8,128)S(1)}, u32[]{:S(2)}, u32[]{:S(2)}) collective-permute-start(f32[6,128]{1,0:T(8,128)S(1)} %get-tuple-element.109), channel_id=1, source_target_pairs={{0,1},{1,2},{2,3},{3,4},{4,5},{5,6},{6,7},{7,8},{8,9},{9,10},{10,1... | collective-permute-start | bytes 9224 | tf_op jit(solution)/shard_map/ppermute | solution.py:14
  476.3 46.5 %collective-permute-start.25 = (f32[6,128]{1,0:T(8,128)S(1)}, f32[6,128]{1,0:T(8,128)S(1)}, u32[]{:S(2)}, u32[]{:S(2)}) collective-permute-start(f32[6,128]{1,0:T(8,128)S(1)} %get-tuple-element.112), channel_id=1, source_target_pairs={{0,9},{1,10},{2,11},{3,12},{4,13},{5,14},{6,15},{7,16},{8,17},{9,1... | collective-permute-start | bytes 9224 | tf_op jit(solution)/shard_map/ppermute | solution.py:14
  478.7 44.2 %collective-permute-start.26 = (f32[6,128]{1,0:T(8,128)S(1)}, f32[6,128]{1,0:T(8,128)S(1)}, u32[]{:S(2)}, u32[]{:S(2)}) collective-permute-start(f32[6,128]{1,0:T(8,128)S(1)} %get-tuple-element.111), channel_id=1, source_target_pairs={{0,8},{1,9},{2,10},{3,11},{4,12},{5,13},{6,14},{7,15},{8,16},{9,17... | collective-permute-start | bytes 9224 | tf_op jit(solution)/shard_map/ppermute | solution.py:14
  480.9 42.0 %collective-permute-start.27 = (f32[6,128]{1,0:T(8,128)S(1)}, f32[6,128]{1,0:T(8,128)S(1)}, u32[]{:S(2)}, u32[]{:S(2)}) collective-permute-start(f32[6,128]{1,0:T(8,128)S(1)} %get-tuple-element.110), channel_id=1, source_target_pairs={{0,7},{1,8},{2,9},{3,10},{4,11},{5,12},{6,13},{7,14},{8,15},{9,16}... | collective-permute-start | bytes 9224 | tf_op jit(solution)/shard_map/ppermute | solution.py:14
  (74 other events, 2153.3 us)
where the time goes:
time: 539 us; the launch traced here: 529 us
  other arithmetic  154 us (29%)
  blocking collectives  143 us (27%)
  local copies, waits for them, and re-layouts  138 us (26%)
  starting transfers between devices  71.9 us (13%)
  waiting for transfers between devices  11.1 us (2%)
  between operations  10.8 us (2%)
    psum x2, blocking collectives, sum_pairs(): return lax.psum((first_term, second_term), ('gx', 'gy'))  143 us
    scatter-add x3, other arithmetic, spread(): loads = jnp.zeros((6, seg_rows), jnp.float32).at[:, all_rows].add(pushes)  101 us
    gather x8, local copies, waits for them, and re-layouts, picked(): taken = jnp.take(source, all_rows, axis=1)  91.8 us
    ppermute x28, starting transfers between devices, passed_along(): return lax.ppermute(shard, axis, pairs)  71.9 us
    scatter-add x3, other arithmetic, spread(): jnp.zeros((6, 4 * export_cap), jnp.float32).at[:, slot_flat].add(cross_two)  18.5 us
    gather x8, local copies, waits for them, and re-layouts, incoming(): return jnp.take(flattened, slot_flat, axis=1)  12.5 us
    scatter-add x3, other arithmetic, spread(): loads.at[:, export_flat].add(jnp.moveaxis(returned, 0, 1).reshape(6, -1))  11.9 us
    ppermute x28, waiting for transfers between devices, passed_along(): return lax.ppermute(shard, axis, pairs)  11.1 us
  transfers between devices with their start and end apart: 28, of which 5 were waited for; matrix products, arithmetic and copies ran while one was open for 35% of the time, Pallas kernels for 0%

commit v1 on v0

--- a/solution.py
+++ b/solution.py
@@ -77,7 +77,7 @@
 
 
 def sum_pairs(first_term, second_term):
-    return lax.psum((first_term, second_term), ("gx", "gy"))
+    return lax.psum(lax.psum((first_term, second_term), "gx"), "gy")
 
 
 def on_device(

time: 539 us -> 497 us (0.922); the launches traced: 529 us -> 493 us
  blocking collectives: 143 us -> 119 us
  starting transfers between devices: 71.9 us -> 61.9 us
    psum x2 -> x4, blocking collectives: 143 us -> 119 us  [sum_pairs(): return lax.psum(lax.psum((first_term, second_term), 'gx'), 'gy')]
    ppermute x28, starting transfers between devices: 71.9 us -> 61.9 us  [passed_along(): return lax.ppermute(shard, axis, pairs)]
  transfers between devices with their start and end apart: 28 -> 28, of which waited for: 5 -> 5; matrix products, arithmetic and copies ran while one was open for 35% -> 37% of each run, Pallas kernels for 0% -> 0%
where the time goes in v1:
time: 497 us; the launch traced here: 493 us
  other arithmetic  154 us (31%)
  local copies, waits for them, and re-layouts  138 us (28%)
  blocking collectives  119 us (24%)
  starting transfers between devices  61.9 us (12%)
  between operations  10.6 us (2%)
  waiting for transfers between devices  9.83 us (2%)
    psum x4, blocking collectives, sum_pairs(): return lax.psum(lax.psum((first_term, second_term), 'gx'), 'gy')  119 us
    scatter-add x3, other arithmetic, spread(): loads = jnp.zeros((6, seg_rows), jnp.float32).at[:, all_rows].add(pushes)  101 us
    gather x8, local copies, waits for them, and re-layouts, picked(): taken = jnp.take(source, all_rows, axis=1)  91.8 us
    ppermute x28, starting transfers between devices, passed_along(): return lax.ppermute(shard, axis, pairs)  61.9 us
    scatter-add x3, other arithmetic, spread(): jnp.zeros((6, 4 * export_cap), jnp.float32).at[:, slot_flat].add(cross_two)  18.5 us
    gather x8, local copies, waits for them, and re-layouts, incoming(): return jnp.take(flattened, slot_flat, axis=1)  12.5 us
    scatter-add x3, other arithmetic, spread(): loads.at[:, export_flat].add(jnp.moveaxis(returned, 0, 1).reshape(6, -1))  11.7 us
  transfers between devices with their start and end apart: 28, of which 5 were waited for; matrix products, arithmetic and copies ran while one was open for 37% of the time, Pallas kernels for 0%

profile of v1, /device:TPU:1, one launch (start us, length us, event | category | flops | bytes accessed | tf_op | source)
XLA Modules:
  0.0 493.3 jit_solution(11638266789849201067)
XLA Ops:
  11.4 3.3 collective-permute-start
  23.0 20.9 %gather_fusion.1 = f32[6144,6]{1,0:T(8,128)} fusion(f32[6,2048]{0,1:T(8,128)S(1)} %copy.319, s32[6144]{0:T(1024)S(1)} %fusion.33), kind=kCustom, calls=%fused_computation.3.clone | custom fusion | bytes 319488 | tf_op jit(solution)/shard_map/jit(_take)/gather | solution.py:121
  43.9 20.9 %gather_fusion = f32[6144,6]{1,0:T(8,128)} fusion(f32[6,2048]{0,1:T(8,128)S(1)} %copy.317, s32[6144]{0:T(1024)S(1)} %fusion.33), kind=kCustom, calls=%fused_computation.clone | custom fusion | bytes 319488 | tf_op jit(solution)/shard_map/jit(_take)/gather | solution.py:121
  88.5 3.3 gather_fusion.3
  94.6 2.8 gather_fusion.5
  100.2 6.1 %scatter_custom_fusion.1 = f32[6,512]{0,1:T(8,128)S(1)} fusion(s32[1024]{0:T(1024)S(1)} %bitcast.296, f32[1024,6]{1,0:T(8,128)S(1)} %copy.336, f32[]{:T(128)} %constant.32.clone.1), kind=kCustom, calls=%fused_computation.39 | custom fusion | flops 6144 | bytes 12292 | tf_op jit(solution)/shard_map/scatter-add | solution.py:153
  106.4 4.1 collective-permute-start.8
  110.4 5.0 %collective-permute-start.9 = (f32[6,128]{1,0:T(8,128)S(1)}, f32[6,128]{1,0:T(8,128)S(1)}, u32[]{:S(2)}, u32[]{:S(2)}) collective-permute-start(f32[6,128]{1,0:T(8,128)S(1)} %get-tuple-element.136), channel_id=1, source_target_pairs={{0,9},{1,10},{2,11},{3,12},{4,13},{5,14},{6,15},{7,16},{8,17},{9,1... | collective-permute-start | bytes 9224 | tf_op jit(solution)/shard_map/ppermute | solution.py:14
  115.5 5.1 %collective-permute-start.10 = (f32[6,128]{1,0:T(8,128)S(1)}, f32[6,128]{1,0:T(8,128)S(1)}, u32[]{:S(2)}, u32[]{:S(2)}) collective-permute-start(f32[6,128]{1,0:T(8,128)S(1)} %get-tuple-element.135), channel_id=1, source_target_pairs={{0,8},{1,9},{2,10},{3,11},{4,12},{5,13},{6,14},{7,15},{8,16},{9,17... | collective-permute-start | bytes 9224 | tf_op jit(solution)/shard_map/ppermute | solution.py:14
  120.6 6.2 %collective-permute-start.11 = (f32[6,128]{1,0:T(8,128)S(1)}, f32[6,128]{1,0:T(8,128)S(1)}, u32[]{:S(2)}, u32[]{:S(2)}) collective-permute-start(f32[6,128]{1,0:T(8,128)S(1)} %get-tuple-element.134), channel_id=1, source_target_pairs={{0,7},{1,8},{2,9},{3,10},{4,11},{5,12},{6,13},{7,14},{8,15},{9,16}... | collective-permute-start | bytes 9224 | tf_op jit(solution)/shard_map/ppermute | solution.py:14
  130.8 33.7 %scatter_custom_fusion = f32[6,2048]{0,1:T(8,128)S(1)} fusion(s32[6144]{0:T(1024)S(1)} %bitcast.275, f32[6144,6]{1,0:T(8,128)} %copy.335, f32[]{:T(128)} %constant.32.clone.1), kind=kCustom, calls=%fused_computation.25 | custom fusion | flops 36864 | bytes 49664 | tf_op jit(solution)/shard_map/scatter-add | solution.py:156
  164.9 3.9 scatter_fusion
  171.5 20.9 %gather_fusion.6 = f32[6144,6]{1,0:T(8,128)} fusion(f32[6,2048]{0,1:T(8,128)S(1)} %copy.344, s32[6144]{0:T(1024)S(1)} %copy-done.4), kind=kCustom, calls=%fused_computation.4.clone | custom fusion | bytes 319488 | tf_op jit(solution)/shard_map/jit(_take)/gather | solution.py:121
  192.6 3.2 collective-permute-start.12
  199.7 2.4 copy.345
  204.0 4.1 collective-permute-done.15
  208.3 2.8 gather_fusion.8
  215.3 39.6 %all-reduce.1 = (f32[]{:T(128)}, f32[]{:T(128)}) all-reduce(f32[]{:T(128)S(6)} %add.318, f32[]{:T(128)S(6)} %add.327), channel_id=1, replica_groups=mesh['gx'=16,'gy'=8] {'gx'}, use_global_device_ids=true, to_apply=%region_11.15 | all-reduce | flops 2 | bytes 16 | tf_op jit(solution)/shard_map/psum | solution.py:80
  254.9 22.2 %all-reduce.3 = (f32[]{:T(128)}, f32[]{:T(128)}) all-reduce(f32[]{:T(128)} %get-tuple-element.48, f32[]{:T(128)} %get-tuple-element.49), channel_id=1, replica_groups=mesh['gx'=16,'gy'=8] {'gy'}, use_global_device_ids=true, to_apply=%region_12.16 | all-reduce | flops 2 | bytes 16 | tf_op jit(solution)/shard_map/psum | solution.py:80
  278.7 6.2 %scatter_custom_fusion.4 = f32[6,512]{0,1:T(8,128)S(1)} fusion(s32[1024]{0:T(1024)} %bitcast.297, f32[1024,6]{1,0:T(8,128)S(1)} %copy.354, f32[]{:T(128)} %constant.32.clone.1), kind=kCustom, calls=%fused_computation.37 | custom fusion | flops 6144 | bytes 12800 | tf_op jit(solution)/shard_map/scatter-add | solution.py:153
  294.1 33.7 %scatter_custom_fusion.3 = f32[6,2048]{0,1:T(8,128)S(1)} fusion(s32[6144]{0:T(1024)} %bitcast.276, f32[6144,6]{1,0:T(8,128)} %copy.353, f32[]{:T(128)} %constant.32.clone.1), kind=kCustom, calls=%fused_computation.23 | custom fusion | flops 36864 | bytes 49664 | tf_op jit(solution)/shard_map/scatter-add | solution.py:156
  328.1 3.9 scatter_fusion.1
  333.7 20.9 %gather_fusion.9 = f32[6144,6]{1,0:T(8,128)} fusion(f32[6,2048]{0,1:T(8,128)S(1)} %copy.362, s32[6144]{0:T(1024)S(1)} %copy-done.4), kind=kCustom, calls=%fused_computation.5.clone | custom fusion | bytes 319488 | tf_op jit(solution)/shard_map/jit(_take)/gather | solution.py:121
  355.9 2.4 copy.363
  358.7 4.4 collective-permute-start.20
  368.9 2.5 collective-permute-done.23
  371.6 2.8 gather_fusion.11
  378.0 34.6 %all-reduce = (f32[]{:T(128)}, f32[]{:T(128)}) all-reduce(f32[]{:T(128)S(6)} %add.329, f32[]{:T(128)S(6)} %add.336), channel_id=1, replica_groups=mesh['gx'=16,'gy'=8] {'gx'}, use_global_device_ids=true, to_apply=%region_29.33 | all-reduce | flops 2 | bytes 16 | tf_op jit(solution)/shard_map/psum | solution.py:80
  412.6 22.6 %all-reduce.2 = (f32[]{:T(128)}, f32[]{:T(128)}) all-reduce(f32[]{:T(128)} %get-tuple-element.46, f32[]{:T(128)} %get-tuple-element.47), channel_id=1, replica_groups=mesh['gx'=16,'gy'=8] {'gy'}, use_global_device_ids=true, to_apply=%region_30.34 | all-reduce | flops 2 | bytes 16 | tf_op jit(solution)/shard_map/psum | solution.py:80
  437.4 6.2 %scatter_custom_fusion.7 = f32[6,512]{0,1:T(8,128)S(1)} fusion(s32[1024]{0:T(1024)} %bitcast.298, f32[1024,6]{1,0:T(8,128)S(1)} %copy.372, f32[]{:T(128)} %constant.32.clone.1), kind=kCustom, calls=%fused_computation.35 | custom fusion | flops 6144 | bytes 12800 | tf_op jit(solution)/shard_map/scatter-add | solution.py:153
  453.5 33.7 %scatter_custom_fusion.6 = f32[6,2048]{0,1:T(8,128)S(1)} fusion(s32[6144]{0:T(1024)} %bitcast.277, f32[6144,6]{1,0:T(8,128)} %copy.371, f32[]{:T(128)} %constant.32.clone.1), kind=kCustom, calls=%fused_computation.21 | custom fusion | flops 36864 | bytes 49664 | tf_op jit(solution)/shard_map/scatter-add | solution.py:156
  487.6 4.0 scatter_fusion.2
  (397 shorter events, 94.4 us)
Async XLA Ops:
  11.4 70.4 %collective-permute-start = (f32[6,128]{1,0:T(8,128)}, f32[6,128]{1,0:T(8,128)}, u32[]{:S(2)}, u32[]{:S(2)}) collective-permute-start(f32[6,128]{1,0:T(8,128)} %get-tuple-element.145), channel_id=1, source_target_pairs={{1,0},{2,1},{3,2},{4,3},{5,4},{6,5},{7,6},{8,7},{9,8},{10,9},{11,1... | collective-permute-start | bytes 9224 | tf_op jit(solution)/shard_map/ppermute | solution.py:14
  14.7 69.1 %collective-permute-start.1 = (f32[6,128]{1,0:T(8,128)}, f32[6,128]{1,0:T(8,128)}, u32[]{:S(2)}, u32[]{:S(2)}) collective-permute-start(f32[6,128]{1,0:T(8,128)} %get-tuple-element.148), channel_id=1, source_target_pairs={{9,0},{10,1},{11,2},{12,3},{13,4},{14,5},{15,6},{16,7},{17,8},{18,... | collective-permute-start | bytes 9224 | tf_op jit(solution)/shard_map/ppermute | solution.py:14
  16.0 69.7 %collective-permute-start.2 = (f32[6,128]{1,0:T(8,128)}, f32[6,128]{1,0:T(8,128)}, u32[]{:S(2)}, u32[]{:S(2)}) collective-permute-start(f32[6,128]{1,0:T(8,128)} %get-tuple-element.147), channel_id=1, source_target_pairs={{8,0},{9,1},{10,2},{11,3},{12,4},{13,5},{14,6},{15,7},{16,8},{17,9... | collective-permute-start | bytes 9224 | tf_op jit(solution)/shard_map/ppermute | solution.py:14
  17.3 70.4 %collective-permute-start.3 = (f32[6,128]{1,0:T(8,128)}, f32[6,128]{1,0:T(8,128)}, u32[]{:S(2)}, u32[]{:S(2)}) collective-permute-start(f32[6,128]{1,0:T(8,128)} %get-tuple-element.146), channel_id=1, source_target_pairs={{7,0},{8,1},{9,2},{10,3},{11,4},{12,5},{13,6},{14,7},{15,8},{16,9}... | collective-permute-start | bytes 9224 | tf_op jit(solution)/shard_map/ppermute | solution.py:14
  19.2 72.9 %collective-permute-start.4 = (f32[6,128]{1,0:T(8,128)}, f32[6,128]{1,0:T(8,128)}, u32[]{:S(2)}, u32[]{:S(2)}) collective-permute-start(f32[6,128]{1,0:T(8,128)} %get-tuple-element.141), channel_id=1, source_target_pairs={{1,0},{2,1},{3,2},{4,3},{5,4},{6,5},{7,6},{8,7},{9,8},{10,9},{11,1... | collective-permute-start | bytes 9224 | tf_op jit(solution)/shard_map/ppermute | solution.py:14
  81.7 11.0 %collective-permute-start.5 = (f32[6,128]{1,0:T(8,128)}, f32[6,128]{1,0:T(8,128)S(1)}, u32[]{:S(2)}, u32[]{:S(2)}) collective-permute-start(f32[6,128]{1,0:T(8,128)} %get-tuple-element.144), channel_id=1, source_target_pairs={{9,0},{10,1},{11,2},{12,3},{13,4},{14,5},{15,6},{16,7},{17,8},{18,... | collective-permute-start | bytes 9224 | tf_op jit(solution)/shard_map/ppermute | solution.py:14
  83.7 9.0 %collective-permute-start.6 = (f32[6,128]{1,0:T(8,128)}, f32[6,128]{1,0:T(8,128)S(1)}, u32[]{:S(2)}, u32[]{:S(2)}) collective-permute-start(f32[6,128]{1,0:T(8,128)} %get-tuple-element.143), channel_id=1, source_target_pairs={{8,0},{9,1},{10,2},{11,3},{12,4},{13,5},{14,6},{15,7},{16,8},{17,9... | collective-permute-start | bytes 9224 | tf_op jit(solution)/shard_map/ppermute | solution.py:14
  85.7 8.7 %collective-permute-start.7 = (f32[6,128]{1,0:T(8,128)}, f32[6,128]{1,0:T(8,128)S(1)}, u32[]{:S(2)}, u32[]{:S(2)}) collective-permute-start(f32[6,128]{1,0:T(8,128)} %get-tuple-element.142), channel_id=1, source_target_pairs={{7,0},{8,1},{9,2},{10,3},{11,4},{12,5},{13,6},{14,7},{15,8},{16,9}... | collective-permute-start | bytes 9224 | tf_op jit(solution)/shard_map/ppermute | solution.py:14
  106.4 58.2 %collective-permute-start.8 = (f32[6,128]{1,0:T(8,128)S(1)}, f32[6,128]{1,0:T(8,128)S(1)}, u32[]{:S(2)}, u32[]{:S(2)}) collective-permute-start(f32[6,128]{1,0:T(8,128)S(1)} %get-tuple-element.133), channel_id=1, source_target_pairs={{0,1},{1,2},{2,3},{3,4},{4,5},{5,6},{6,7},{7,8},{8,9},{9,10},{10,1... | collective-permute-start | bytes 9224 | tf_op jit(solution)/shard_map/ppermute | solution.py:14
  110.4 54.2 %collective-permute-start.9 = (f32[6,128]{1,0:T(8,128)S(1)}, f32[6,128]{1,0:T(8,128)S(1)}, u32[]{:S(2)}, u32[]{:S(2)}) collective-permute-start(f32[6,128]{1,0:T(8,128)S(1)} %get-tuple-element.136), channel_id=1, source_target_pairs={{0,9},{1,10},{2,11},{3,12},{4,13},{5,14},{6,15},{7,16},{8,17},{9,1... | collective-permute-start | bytes 9224 | tf_op jit(solution)/shard_map/ppermute | solution.py:14
  115.5 49.2 %collective-permute-start.10 = (f32[6,128]{1,0:T(8,128)S(1)}, f32[6,128]{1,0:T(8,128)S(1)}, u32[]{:S(2)}, u32[]{:S(2)}) collective-permute-start(f32[6,128]{1,0:T(8,128)S(1)} %get-tuple-element.135), channel_id=1, source_target_pairs={{0,8},{1,9},{2,10},{3,11},{4,12},{5,13},{6,14},{7,15},{8,16},{9,17... | collective-permute-start | bytes 9224 | tf_op jit(solution)/shard_map/ppermute | solution.py:14
  120.6 44.1 %collective-permute-start.11 = (f32[6,128]{1,0:T(8,128)S(1)}, f32[6,128]{1,0:T(8,128)S(1)}, u32[]{:S(2)}, u32[]{:S(2)}) collective-permute-start(f32[6,128]{1,0:T(8,128)S(1)} %get-tuple-element.134), channel_id=1, source_target_pairs={{0,7},{1,8},{2,9},{3,10},{4,11},{5,12},{6,13},{7,14},{8,15},{9,16}... | collective-permute-start | bytes 9224 | tf_op jit(solution)/shard_map/ppermute | solution.py:14
  192.6 11.0 %collective-permute-start.12 = (f32[6,128]{1,0:T(8,128)S(1)}, f32[6,128]{1,0:T(8,128)S(1)}, u32[]{:S(2)}, u32[]{:S(2)}) collective-permute-start(f32[6,128]{1,0:T(8,128)S(1)} %get-tuple-element.129), channel_id=1, source_target_pairs={{1,0},{2,1},{3,2},{4,3},{5,4},{6,5},{7,6},{8,7},{9,8},{10,9},{11,1... | collective-permute-start | bytes 9224 | tf_op jit(solution)/shard_map/ppermute | solution.py:14
  195.8 7.8 %collective-permute-start.13 = (f32[6,128]{1,0:T(8,128)S(1)}, f32[6,128]{1,0:T(8,128)S(1)}, u32[]{:S(2)}, u32[]{:S(2)}) collective-permute-start(f32[6,128]{1,0:T(8,128)S(1)} %get-tuple-element.132), channel_id=1, source_target_pairs={{9,0},{10,1},{11,2},{12,3},{13,4},{14,5},{15,6},{16,7},{17,8},{18,... | collective-permute-start | bytes 9224 | tf_op jit(solution)/shard_map/ppermute | solution.py:14
  197.1 6.9 %collective-permute-start.14 = (f32[6,128]{1,0:T(8,128)S(1)}, f32[6,128]{1,0:T(8,128)S(1)}, u32[]{:S(2)}, u32[]{:S(2)}) collective-permute-start(f32[6,128]{1,0:T(8,128)S(1)} %get-tuple-element.131), channel_id=1, source_target_pairs={{8,0},{9,1},{10,2},{11,3},{12,4},{13,5},{14,6},{15,7},{16,8},{17,9... | collective-permute-start | bytes 9224 | tf_op jit(solution)/shard_map/ppermute | solution.py:14
  198.4 93.2 %copy-start.49 = (f32[1,2560]{1,0:T(1,128)S(1)}, f32[1,2560]{1,0:T(1,128)}, u32[]{:S(2)}) copy-start(f32[1,2560]{1,0:T(1,128)} %get-tuple-element.65) | copy-start | bytes 30724
  198.4 9.7 %collective-permute-start.15 = (f32[6,128]{1,0:T(8,128)S(1)}, f32[6,128]{1,0:T(8,128)S(1)}, u32[]{:S(2)}, u32[]{:S(2)}) collective-permute-start(f32[6,128]{1,0:T(8,128)S(1)} %get-tuple-element.130), channel_id=1, source_target_pairs={{7,0},{8,1},{9,2},{10,3},{11,4},{12,5},{13,6},{14,7},{15,8},{16,9}... | collective-permute-start | bytes 9224 | tf_op jit(solution)/shard_map/ppermute | solution.py:14
  285.0 42.8 %collective-permute-start.16 = (f32[6,128]{1,0:T(8,128)S(1)}, f32[6,128]{1,0:T(8,128)S(1)}, u32[]{:S(2)}, u32[]{:S(2)}) collective-permute-start(f32[6,128]{1,0:T(8,128)S(1)} %get-tuple-element.123), channel_id=1, source_target_pairs={{0,1},{1,2},{2,3},{3,4},{4,5},{5,6},{6,7},{7,8},{8,9},{9,10},{10,1... | collective-permute-start | bytes 9224 | tf_op jit(solution)/shard_map/ppermute | solution.py:14
  287.0 40.9 %collective-permute-start.17 = (f32[6,128]{1,0:T(8,128)S(1)}, f32[6,128]{1,0:T(8,128)S(1)}, u32[]{:S(2)}, u32[]{:S(2)}) collective-permute-start(f32[6,128]{1,0:T(8,128)S(1)} %get-tuple-element.126), channel_id=1, source_target_pairs={{0,9},{1,10},{2,11},{3,12},{4,13},{5,14},{6,15},{7,16},{8,17},{9,1... | collective-permute-start | bytes 9224 | tf_op jit(solution)/shard_map/ppermute | solution.py:14
  288.3 39.6 %collective-permute-start.18 = (f32[6,128]{1,0:T(8,128)S(1)}, f32[6,128]{1,0:T(8,128)S(1)}, u32[]{:S(2)}, u32[]{:S(2)}) collective-permute-start(f32[6,128]{1,0:T(8,128)S(1)} %get-tuple-element.125), channel_id=1, source_target_pairs={{0,8},{1,9},{2,10},{3,11},{4,12},{5,13},{6,14},{7,15},{8,16},{9,17... | collective-permute-start | bytes 9224 | tf_op jit(solution)/shard_map/ppermute | solution.py:14
  289.6 38.4 %collective-permute-start.19 = (f32[6,128]{1,0:T(8,128)S(1)}, f32[6,128]{1,0:T(8,128)S(1)}, u32[]{:S(2)}, u32[]{:S(2)}) collective-permute-start(f32[6,128]{1,0:T(8,128)S(1)} %get-tuple-element.124), channel_id=1, source_target_pairs={{0,7},{1,8},{2,9},{3,10},{4,11},{5,12},{6,13},{7,14},{8,15},{9,16}... | collective-permute-start | bytes 9224 | tf_op jit(solution)/shard_map/ppermute | solution.py:14
  355.9 94.5 %copy-start.50 = (f32[1,2560]{1,0:T(1,128)S(1)}, f32[1,2560]{1,0:T(1,128)}, u32[]{:S(2)}) copy-start(f32[1,2560]{1,0:T(1,128)} %get-tuple-element.65) | copy-start | bytes 30724
  355.9 94.5 %copy-start.55 = (f32[1,2560]{1,0:T(1,128)S(1)}, f32[1,2560]{1,0:T(1,128)}, u32[]{:S(2)}) copy-start(f32[1,2560]{1,0:T(1,128)} %get-tuple-element.66) | copy-start | bytes 30724
  358.3 92.3 %copy-start.67 = (f32[1,4,256]{2,1,0:T(4,128)S(1)}, f32[1,4,256]{2,1,0:T(4,128)}, u32[]{:S(2)}) copy-start(f32[1,4,256]{2,1,0:T(4,128)} %sqrt.64) | copy-start | bytes 12292
  358.7 9.0 %collective-permute-start.20 = (f32[6,128]{1,0:T(8,128)S(1)}, f32[6,128]{1,0:T(8,128)S(1)}, u32[]{:S(2)}, u32[]{:S(2)}) collective-permute-start(f32[6,128]{1,0:T(8,128)S(1)} %get-tuple-element.119), channel_id=1, source_target_pairs={{1,0},{2,1},{3,2},{4,3},{5,4},{6,5},{7,6},{8,7},{9,8},{10,9},{11,1... | collective-permute-start | bytes 9224 | tf_op jit(solution)/shard_map/ppermute | solution.py:14
  363.1 5.8 %collective-permute-start.21 = (f32[6,128]{1,0:T(8,128)S(1)}, f32[6,128]{1,0:T(8,128)S(1)}, u32[]{:S(2)}, u32[]{:S(2)}) collective-permute-start(f32[6,128]{1,0:T(8,128)S(1)} %get-tuple-element.122), channel_id=1, source_target_pairs={{9,0},{10,1},{11,2},{12,3},{13,4},{14,5},{15,6},{16,7},{17,8},{18,... | collective-permute-start | bytes 9224 | tf_op jit(solution)/shard_map/ppermute | solution.py:14
  364.4 4.5 collective-permute-start.22
  365.7 5.7 %collective-permute-start.23 = (f32[6,128]{1,0:T(8,128)S(1)}, f32[6,128]{1,0:T(8,128)S(1)}, u32[]{:S(2)}, u32[]{:S(2)}) collective-permute-start(f32[6,128]{1,0:T(8,128)S(1)} %get-tuple-element.120), channel_id=1, source_target_pairs={{7,0},{8,1},{9,2},{10,3},{11,4},{12,5},{13,6},{14,7},{15,8},{16,9}... | collective-permute-start | bytes 9224 | tf_op jit(solution)/shard_map/ppermute | solution.py:14
  443.8 43.5 %collective-permute-start.24 = (f32[6,128]{1,0:T(8,128)S(1)}, f32[6,128]{1,0:T(8,128)S(1)}, u32[]{:S(2)}, u32[]{:S(2)}) collective-permute-start(f32[6,128]{1,0:T(8,128)S(1)} %get-tuple-element.113), channel_id=1, source_target_pairs={{0,1},{1,2},{2,3},{3,4},{4,5},{5,6},{6,7},{7,8},{8,9},{9,10},{10,1... | collective-permute-start | bytes 9224 | tf_op jit(solution)/shard_map/ppermute | solution.py:14
  445.7 41.6 %collective-permute-start.25 = (f32[6,128]{1,0:T(8,128)S(1)}, f32[6,128]{1,0:T(8,128)S(1)}, u32[]{:S(2)}, u32[]{:S(2)}) collective-permute-start(f32[6,128]{1,0:T(8,128)S(1)} %get-tuple-element.116), channel_id=1, source_target_pairs={{0,9},{1,10},{2,11},{3,12},{4,13},{5,14},{6,15},{7,16},{8,17},{9,1... | collective-permute-start | bytes 9224 | tf_op jit(solution)/shard_map/ppermute | solution.py:14
  447.0 40.4 %collective-permute-start.26 = (f32[6,128]{1,0:T(8,128)S(1)}, f32[6,128]{1,0:T(8,128)S(1)}, u32[]{:S(2)}, u32[]{:S(2)}) collective-permute-start(f32[6,128]{1,0:T(8,128)S(1)} %get-tuple-element.115), channel_id=1, source_target_pairs={{0,8},{1,9},{2,10},{3,11},{4,12},{5,13},{6,14},{7,15},{8,16},{9,17... | collective-permute-start | bytes 9224 | tf_op jit(solution)/shard_map/ppermute | solution.py:14
  448.3 39.1 %collective-permute-start.27 = (f32[6,128]{1,0:T(8,128)S(1)}, f32[6,128]{1,0:T(8,128)S(1)}, u32[]{:S(2)}, u32[]{:S(2)}) collective-permute-start(f32[6,128]{1,0:T(8,128)S(1)} %get-tuple-element.114), channel_id=1, source_target_pairs={{0,7},{1,8},{2,9},{3,10},{4,11},{5,12},{6,13},{7,14},{8,15},{9,16}... | collective-permute-start | bytes 9224 | tf_op jit(solution)/shard_map/ppermute | solution.py:14
  (74 other events, 2047.4 us)
